TPU v7x, 32 devices: a whole 2x2x4 slice. The times are simulated.
32 devices in a mesh: dp: 2 (over y), seq: 16 (over z, x, core).
Axes of the slice: x: 2, y: 2, z: 4, core: 2. Of those that a mesh axis runs over, the one named last changes fastest.
Arguments:
- tokens: bfloat16 [2, 8192, 1024], P('dp', 'seq'), may hold values from -50 to 50
- w_query: bfloat16 [1024, 1024], P(None, 'dp'), may hold values from -0.1875 to 0.1875
- w_key: bfloat16 [1024, 1024], P(None, 'dp'), may hold values from -0.1875 to 0.1875
- w_value: bfloat16 [1024, 1024], P(None, 'dp'), may hold values from -0.1875 to 0.1875
- w_out: bfloat16 [1024, 1024], P('dp'), may hold values from -0.1875 to 0.1875
- norm_gain: float32 [1024], replicated, may hold values from 0.1 to 1.9
Outputs:
- layer_out: bfloat16 [2, 8192, 1024], P('dp', 'seq')
All inputs are finite; a program needn't handle non-finite values.
Results may differ from a plain program's by a relative error of at most 0.017.
Values may be sent and summed in bfloat16 or wider, within the bound.
A program may use at most 128 MiB of HBM per device.

v0:
```python
import jax
import jax.numpy as jnp
from jax import lax
from jax.sharding import PartitionSpec as P

H = 8
DH = 128


def entering(value, axis, join, neutral):
    place = lax.axis_index(axis)
    gathered = lax.all_gather(value.astype(jnp.bfloat16), axis)
    state = jnp.zeros_like(value) + jnp.asarray(neutral, value.dtype)

    def one(lap, state):
        return join(state, lax.dynamic_index_in_dim(gathered, lap, 0, False).astype(value.dtype))

    return lax.fori_loop(0, place, one, state)


def inner_block(query_heads, key_heads, value_heads):
    length = query_heads.shape[1]
    block = min(length, 512)
    scores = jnp.einsum("hid,hjd->hij", query_heads, key_heads, preferred_element_type=jnp.float32)
    row_ids = jnp.arange(0, block)[:, None]
    col_ids = jnp.arange(block)[None, :]
    scores = jnp.where(col_ids <= row_ids, scores, 0.0).astype(jnp.bfloat16)
    pieces = jnp.einsum("hij,hje->hie", scores, value_heads, preferred_element_type=jnp.float32)
    return pieces


def add_states(earlier, later):
    return earlier + later


def key_value_state(key_heads, value_heads):
    return jnp.einsum("htd,hte->hde", key_heads, value_heads, preferred_element_type=jnp.float32)


def attend(query_heads, key_heads, value_heads, prior):
    within = inner_block(query_heads, key_heads, value_heads)
    carried = jnp.einsum(
        "htd,hde->hte", query_heads, prior.astype(jnp.bfloat16), preferred_element_type=jnp.float32
    )
    return within + carried


def body(tokens, w_query, w_key, w_value, w_out, norm_gain):
    rows = tokens[0]
    length = rows.shape[0]
    stacked = jnp.stack([w_query, w_key, w_value], axis=0)
    projected = jnp.einsum(
        "td,pdc->ptc",
        rows,
        lax.all_gather(stacked, "dp", axis=2, tiled=True),
        preferred_element_type=jnp.float32,
    ).astype(jnp.bfloat16)
    query = projected[0]
    key = projected[1]
    value = projected[2]
    query_heads = query.reshape(length, H, DH).transpose(1, 0, 2)
    key_heads = key.reshape(length, H, DH).transpose(1, 0, 2)
    value_heads = value.reshape(length, H, DH).transpose(1, 0, 2)
    local_state = key_value_state(key_heads, value_heads)
    empty_state = jnp.zeros((H, DH, DH), jnp.float32)
    prior = entering(local_state, "seq", add_states, empty_state)
    mixed_raw = attend(query_heads, key_heads, value_heads, prior)
    scale = lax.rsqrt(jnp.mean(mixed_raw * mixed_raw, axis=-1, keepdims=True) + 1e-05)
    normed = (mixed_raw * scale * norm_gain.reshape(H, 1, DH)).astype(jnp.bfloat16)
    normed = normed.transpose(1, 0, 2).reshape(length, H * DH)
    result = jnp.dot(
        normed, lax.all_gather(w_out, "dp", axis=0, tiled=True), preferred_element_type=jnp.float32
    )
    return result.astype(jnp.bfloat16)[None]


def solution(mesh):
    in_specs = (
        P("dp", "seq", None),
        P(None, "dp"),
        P(None, "dp"),
        P(None, "dp"),
        P("dp", None),
        P(),
    )
    out_specs = P("dp", "seq", None)
    return jax.shard_map(body, mesh=mesh, in_specs=in_specs, out_specs=out_specs, check_vma=False)
```

profile of v0, /device:TPU:0, one launch (start us, length us, event | category | flops | bytes accessed | tf_op | source)
XLA Modules:
  0.0 202.5 jit_solution(4533514288469171736)
XLA Ops:
  6.5 0.0 copy-start
  6.5 0.0 all-gather.5.cloned.1.call-start
  6.5 1.6 copy.13
  8.1 1.5 copy.14
  9.6 2.3 %copy.15 = bf16[1024,512]{0,1:T(8,128)(2,1)} copy(bf16[1024,512]{1,0:T(8,128)(2,1)} %param.11) | data formatting | bytes 2097152 | tf_op args[3]
  11.9 3.3 %pad_maximum_fusion = bf16[3,1024,512]{1,2,0:T(8,128)(2,1)} fusion(bf16[1,1024,512]{1,2,0:T(8,128)(2,1)} %bitcast.57, bf16[1,1024,512]{1,2,0:T(8,128)(2,1)S(1)} %bitcast.56, bf16[1,1024,512]{1,2,0:T(8,128)(2,1)S(1)} %bitcast.55), kind=kLoop, calls=%fused_computation.6 | loop fusion | flops 3145728 | bytes 6291456 | tf_op jit(solution)/shard_map/stack | solution.py:51
  15.2 0.0 all-gather.5.cloned.1.call-update
  15.2 0.0 all-gather.9.cloned.1.call-start
  15.2 83.2 %all-gather.5.cloned.1.call-done = bf16[3,1024,1024]{1,2,0:T(8,128)(2,1)} async-done(((bf16[3,1024,512]{1,2,0:T(8,128)(2,1)}), bf16[3,1024,1024]{1,2,0:T(8,128)(2,1)}) %all-gather.5.cloned.1.call-update) | async-done | bytes 6291472 | tf_op jit(solution)/shard_map/all_gather | solution.py:55
  98.4 0.0 copy-done
  98.4 6.5 %convert_bitcast_fusion = bf16[3,512,1024]{1,2,0:T(8,128)(2,1)S(1)} fusion(bf16[3,1024,1024]{1,2,0:T(8,128)(2,1)} %all-gather.5.cloned.1.call-done, bf16[1,512,1024]{2,1,0:T(8,128)(2,1)S(1)} %copy-done), kind=kOutput, calls=%fused_computation.7 | convolution fusion | flops 3222798336 | bytes 10485760 | tf_op jit(solution)/shard_map/td,pdc->ptc/dot_general | solution.py:52
  104.9 1.2 fusion.14
  106.1 0.0 copy-start.1
  106.1 1.1 copy-done.1
  107.1 1.2 convolution_convert_fusion.1
  108.3 0.0 all-gather.9.cloned.1.call-update
  108.3 0.0 all-gather.7.cloned.1.call-start
  108.4 0.7 all-gather.7.cloned.1.call-update
  109.1 0.1 iota_compare_fusion
  109.2 1.6 copy.16
  110.8 5.1 %fusion = f32[8,512,128]{1,2,0:T(8,128)} fusion(bf16[8,512,128]{1,2,0:T(8,128)(2,1)S(1)} %bitcast.50, pred[512,512]{1,0:T(8,128)(4,1)S(1)} %iota_compare_fusion, bf16[8,512,128]{1,2,0:T(8,128)(2,1)} %bitcast.52, bf16[512,8,128]{2,0,1:T(8,128)(2,1)S(1)} %copy.16), kind=kOutput, calls=%fused_computation.2 | convolution fusion | flops 1077936128 | bytes 5505024 | tf_op jit(solution)/shard_map/hij,hje->hie/dot_general | solution.py:28
  115.9 43.0 %all-gather.9.cloned.1.call-done = bf16[128,128,128]{2,1,0:T(8,128)(2,1)} async-done(((bf16[8,128,128]{2,1,0:T(8,128)(2,1)}), bf16[128,128,128]{2,1,0:T(8,128)(2,1)}) %all-gather.9.cloned.1.call-update) | async-done | bytes 4194320 | tf_op jit(solution)/shard_map/all_gather | solution.py:12
  159.0 0.0 copy-start.2
  159.0 2.1 %multiply_reduce_fusion = (f32[8,512]{1,0:T(8,128)S(1)}, f32[8,512,128]{1,2,0:T(8,128)S(1)}) fusion(f32[8,512,128]{1,2,0:T(8,128)} %fusion, f32[8,128,128]{2,1,0:T(8,128)S(1)} %get-tuple-element.28, bf16[512,8,128]{2,0,1:T(8,128)(2,1)S(1)} %copy.16), kind=kOutput, calls=%fused_computation.11 | convolution fusion | flops 135917568 | bytes 5783552 | tf_op jit(solution)/shard_map/htd,hde->hte/dot_general | solution.py:42
  161.1 0.0 copy-done.2
  161.1 0.3 fusion.6
  161.4 30.7 %all-gather.7.cloned.1.call-done = bf16[1024,1024]{1,0:T(8,128)(2,1)} async-done(((bf16[512,1024]{1,0:T(8,128)(2,1)}), bf16[1024,1024]{1,0:T(8,128)(2,1)}) %all-gather.7.cloned.1.call-update) | async-done | bytes 2097168 | tf_op jit(solution)/shard_map/all_gather | solution.py:72
  192.1 3.8 %fusion.7 = bf16[1,512,1024]{2,1,0:T(8,128)(2,1)} fusion(bf16[512,1024]{0,1:T(8,128)(2,1)S(1)} %bitcast.54, bf16[1024,1024]{1,0:T(8,128)(2,1)} %all-gather.7.cloned.1.call-done), kind=kOutput, calls=%fused_computation.14 | convolution fusion | flops 1074266112 | bytes 4194304 | tf_op jit(solution)/shard_map/dot_general | solution.py:71
  (3 shorter events, 0.1 us)
Async XLA Ops:
  6.5 91.9 %copy-start = (bf16[1,512,1024]{2,1,0:T(8,128)(2,1)S(1)}, bf16[1,512,1024]{2,1,0:T(8,128)(2,1)}, u32[]{:S(2)}) copy-start(bf16[1,512,1024]{2,1,0:T(8,128)(2,1)} %param.8) | copy-start | bytes 3145732
  6.5 91.9 %all-gather.5.cloned.1.call-start = ((), (), s32[]{:S(2)}) async-start(), calls=%async_computation | async-start | bytes 9437184 | tf_op jit(solution)/shard_map/all_gather | solution.py:55
  15.2 143.7 %all-gather.9.cloned.1.call-start = ((), (), s32[]{:S(2)}) async-start(), calls=%async_computation.2 | async-start | bytes 4456448 | tf_op jit(solution)/shard_map/all_gather | solution.py:12
  106.1 1.1 copy-start.1
  108.3 83.8 %all-gather.7.cloned.1.call-start = ((), (), s32[]{:S(2)}) async-start(), calls=%async_computation.1 | async-start | bytes 3145728 | tf_op jit(solution)/shard_map/all_gather | solution.py:72
  159.0 2.1 %copy-start.2 = (f32[1024]{0:T(1024)S(1)}, f32[1024]{0:T(1024)}, u32[]{:S(2)}) copy-start(f32[1024]{0:T(1024)} %param.13) | copy-start | bytes 12292
Sparse Core Ops, SparseCore 0:
  15.3 83.0 all-gather.4
  108.5 50.3 all-gather.8
  160.5 31.6 all-gather.6
where the time goes:
time: 203 us; the launch traced here: 202 us
  waiting for transfers between devices  158 us (78%)
  matrix products  18.7 us (9%)
  between operations  13.2 us (7%)
  local copies, waits for them, and re-layouts  9.22 us (5%)
  other arithmetic  3.68 us (2%)
    all_gather x1, waiting for transfers between devices, body(): lax.all_gather(stacked, 'dp', axis=2, tiled=True)  83.2 us
    all_gather x1, waiting for transfers between devices, entering(): gathered = lax.all_gather(value.astype(jnp.bfloat16), axis)  43 us
    all_gather x1, waiting for transfers between devices, body(): lax.all_gather(w_out, 'dp', axis=0, tiled=True)  30.7 us
    dot_general x1, matrix products, body(): jnp.einsum('td,pdc->ptc', rows, lax.all_gather(stacked, 'dp', axis=2, til...  6.49 us
    unnamed x9, local copies, waits for them, and re-layouts  6.4 us
    dot_general x1, matrix products, inner_block(): jnp.einsum('hij,hje->hie', scores, value_heads, preferred_element_type=jn...  5.12 us
  transfers between devices with their start and end apart: 3, of which 3 were waited for; matrix products, arithmetic and copies ran while one was open for 5% of the time, Pallas kernels for 0%

commit v1 on v0

--- a/solution.py
+++ b/solution.py
@@ -5,6 +5,21 @@
 
 H = 8
 DH = 128
+
+
+def on_each_block(value, axis, dim, make, out_dim):
+    ways, here, step = (lax.axis_size(axis), lax.axis_index(axis), value.shape[dim])
+    results = []
+    for far in range(ways):
+        arriving = (
+            lax.ppermute(value, axis, [(d, (d + 1) % ways) for d in range(ways)])
+            if far + 1 < ways
+            else value
+        )
+        results.append(make(value, (here - far) % ways * step))
+        value = arriving
+    line = jnp.concatenate(results[::-1], axis=out_dim)
+    return jnp.roll(line, (here + 1) * results[0].shape[out_dim], axis=out_dim)
 
 
 def entering(value, axis, join, neutral):
@@ -49,11 +64,14 @@
     rows = tokens[0]
     length = rows.shape[0]
     stacked = jnp.stack([w_query, w_key, w_value], axis=0)
-    projected = jnp.einsum(
-        "td,pdc->ptc",
-        rows,
-        lax.all_gather(stacked, "dp", axis=2, tiled=True),
-        preferred_element_type=jnp.float32,
+    projected = on_each_block(
+        stacked,
+        "dp",
+        2,
+        lambda shard, offset: jnp.einsum(
+            "td,pdc->ptc", rows, shard, preferred_element_type=jnp.float32
+        ),
+        2,
     ).astype(jnp.bfloat16)
     query = projected[0]
     key = projected[1]

time: 203 us -> 196 us (0.966)
  waiting for transfers between devices: 158 us -> 141 us
  other arithmetic: 3.68 us -> 9.54 us
  starting transfers between devices: 0.09 us -> 3.04 us
    all_gather x1 -> x0, waiting for transfers between devices: 83.2 us -> none  [body(): lax.all_gather(stacked, 'dp', axis=2, tiled=True)]
    ppermute x0 -> x1, waiting for transfers between devices: none -> 65.3 us  [on_each_block(): lax.ppermute(value, axis, [(d, (d + 1) % ways) for d in range(ways)])]
    convert_element_type x0 -> x1, other arithmetic: none -> 5.94 us  [body(): projected = on_each_block(stacked, 'dp', 2, lambda shard, offset: jnp.ein...]
    ppermute x0 -> x1, starting transfers between devices: none -> 3 us  [on_each_block(): lax.ppermute(value, axis, [(d, (d + 1) % ways) for d in range(ways)])]
    dot_general x1 -> x2, matrix products: 6.49 us -> 6.78 us  [body(): jnp.einsum('td,pdc->ptc', rows, shard, preferred_element_type=jnp.float32)]
  transfers between devices with their start and end apart: 3 -> 3, of which waited for: 3 -> 3; matrix products, arithmetic and copies ran while one was open for 5% -> 6% of each run, Pallas kernels for 0% -> 0%
where the time goes in v1:
time: 196 us; the launch traced here: 195 us
  waiting for transfers between devices  141 us (72%)
  matrix products  19 us (10%)
  between operations  13.5 us (7%)
  other arithmetic  9.54 us (5%)
  local copies, waits for them, and re-layouts  9.23 us (5%)
  starting transfers between devices  3.04 us (2%)
    ppermute x1, waiting for transfers between devices, on_each_block(): lax.ppermute(value, axis, [(d, (d + 1) % ways) for d in range(ways)])  65.3 us
    all_gather x1, waiting for transfers between devices, entering(): gathered = lax.all_gather(value.astype(jnp.bfloat16), axis)  44.4 us
    all_gather x1, waiting for transfers between devices, body(): lax.all_gather(w_out, 'dp', axis=0, tiled=True)  30.7 us
    dot_general x2, matrix products, body(): jnp.einsum('td,pdc->ptc', rows, shard, preferred_element_type=jnp.float32)  6.78 us
    unnamed x9, local copies, waits for them, and re-layouts  6.41 us
    convert_element_type x1, other arithmetic, body(): projected = on_each_block(stacked, 'dp', 2, lambda shard, offset: jnp.ein...  5.94 us
    dot_general x1, matrix products, inner_block(): jnp.einsum('hij,hje->hie', scores, value_heads, preferred_element_type=jn...  5.13 us
  transfers between devices with their start and end apart: 3, of which 3 were waited for; matrix products, arithmetic and copies ran while one was open for 6% of the time, Pallas kernels for 0%

profile of v1, /device:TPU:0, one launch (start us, length us, event | category | flops | bytes accessed | tf_op | source)
XLA Modules:
  0.0 195.5 jit_solution(4400005106560650813)
XLA Ops:
  6.5 0.0 copy-start
  6.5 0.0 all-gather.6.cloned.1.call-start
  6.5 1.6 copy.13
  8.1 1.5 copy.14
  9.6 2.3 %copy.15 = bf16[1024,512]{0,1:T(8,128)(2,1)} copy(bf16[1024,512]{1,0:T(8,128)(2,1)} %param.11) | data formatting | bytes 2097152 | tf_op args[3]
  11.9 3.2 %pad_maximum_fusion = bf16[3,1024,512]{1,2,0:T(8,128)(2,1)} fusion(bf16[1,1024,512]{1,2,0:T(8,128)(2,1)} %bitcast.57, bf16[1,1024,512]{1,2,0:T(8,128)(2,1)S(1)} %bitcast.55, bf16[1,1024,512]{1,2,0:T(8,128)(2,1)S(1)} %bitcast.53), kind=kLoop, calls=%fused_computation.14 | loop fusion | flops 3145728 | bytes 6291456 | tf_op jit(solution)/shard_map/stack | solution.py:66
  15.1 3.0 %collective-permute-start = (bf16[3,1024,512]{1,2,0:T(8,128)(2,1)}, bf16[3,1024,512]{1,2,0:T(8,128)(2,1)}, u32[]{:S(2)}, u32[]{:S(2)}) collective-permute-start(bf16[3,1024,512]{1,2,0:T(8,128)(2,1)} %pad_maximum_fusion), channel_id=1, source_target_pairs={{0,16},{16,0},{1,17},{17,1},{2,18},{18,2},{3,19},{19,3},{4,20},{20... | collective-permute-start | bytes 9437192 | tf_op jit(solution)/shard_map/ppermute | solution.py:15
  18.1 0.0 copy-done
  18.1 3.1 %convolution_bitcast_fusion = bf16[3,512,512]{1,2,0:T(8,128)(2,1)S(1)} fusion(bf16[1,512,1024]{2,1,0:T(8,128)(2,1)S(1)} %copy-done, bf16[1,1024,512]{1,2,0:T(8,128)(2,1)} %bitcast.58, bf16[1,1024,512]{1,2,0:T(8,128)(2,1)S(1)} %bitcast.56, bf16[1,1024,512]{1,2,0:T(8,128)(2,1)S(1)} %bitcast.54), kind=kOutput, calls=%fused_computation.19 | convolution fusion | flops 1613758464 | bytes 5767168 | tf_op jit(solution)/shard_map/td,pdc->ptc/dot_general | solution.py:71
  21.1 65.3 %collective-permute-done = bf16[3,1024,512]{1,2,0:T(8,128)(2,1)} collective-permute-done((bf16[3,1024,512]{1,2,0:T(8,128)(2,1)}, bf16[3,1024,512]{1,2,0:T(8,128)(2,1)}, u32[]{:S(2)}, u32[]{:S(2)}) %collective-permute-start) | collective-permute-done | bytes 3145760 | tf_op jit(solution)/shard_map/ppermute | solution.py:15
  86.5 3.7 %convolution_bitcast_fusion.1 = bf16[3,512,512]{1,2,0:T(8,128)(2,1)S(1)} fusion(bf16[3,1024,512]{1,2,0:T(8,128)(2,1)} %collective-permute-done, bf16[1,512,1024]{2,1,0:T(8,128)(2,1)S(1)} %copy-done), kind=kOutput, calls=%fused_computation.20 | convolution fusion | flops 1610612736 | bytes 5767168 | tf_op jit(solution)/shard_map/td,pdc->ptc/dot_general | solution.py:71
  90.2 5.9 %fusion.3 = bf16[3,512,1024]{1,2,0:T(8,128)(2,1)S(1)} fusion(s32[]{:T(128)S(6)} %select_n.22, bf16[3,512,512]{1,2,0:T(8,128)(2,1)S(1)} %convolution_bitcast_fusion.1, bf16[3,512,512]{1,2,0:T(8,128)(2,1)S(1)} %convolution_bitcast_fusion), kind=kLoop, calls=%fused_computation.9 | loop fusion | flops 12582912 | bytes 6291460 | tf_op jit(solution)/shard_map/convert_element_type | solution.py:75
  96.2 1.2 fusion.19
  97.3 0.0 copy-start.1
  97.3 1.1 copy-done.1
  98.4 1.2 convolution_convert_fusion.1
  99.6 0.0 all-gather.6.cloned.1.call-update
  99.6 0.0 all-gather.4.cloned.1.call-start
  99.6 0.7 all-gather.4.cloned.1.call-update
  100.4 0.1 iota_compare_fusion
  100.4 1.6 copy.16
  102.1 5.1 %fusion.4 = f32[8,512,128]{1,2,0:T(8,128)} fusion(bf16[8,512,128]{1,2,0:T(8,128)(2,1)S(1)} %bitcast.60, pred[512,512]{1,0:T(8,128)(4,1)S(1)} %iota_compare_fusion, bf16[8,512,128]{1,2,0:T(8,128)(2,1)} %bitcast.62, bf16[512,8,128]{2,0,1:T(8,128)(2,1)S(1)} %copy.16), kind=kOutput, calls=%fused_computation.10 | convolution fusion | flops 1077936128 | bytes 5505024 | tf_op jit(solution)/shard_map/hij,hje->hie/dot_general | solution.py:43
  107.2 44.4 %all-gather.6.cloned.1.call-done = bf16[128,128,128]{2,1,0:T(8,128)(2,1)} async-done(((bf16[8,128,128]{2,1,0:T(8,128)(2,1)}), bf16[128,128,128]{2,1,0:T(8,128)(2,1)}) %all-gather.6.cloned.1.call-update) | async-done | bytes 4194320 | tf_op jit(solution)/shard_map/all_gather | solution.py:27
  151.7 0.0 copy-start.2
  151.7 2.1 %multiply_reduce_fusion = (f32[8,512]{1,0:T(8,128)S(1)}, f32[8,512,128]{1,2,0:T(8,128)S(1)}) fusion(f32[8,512,128]{1,2,0:T(8,128)} %fusion.4, f32[8,128,128]{2,1,0:T(8,128)S(1)} %get-tuple-element.28, bf16[512,8,128]{2,0,1:T(8,128)(2,1)S(1)} %copy.16), kind=kOutput, calls=%fused_computation.18 | convolution fusion | flops 135917568 | bytes 5783552 | tf_op jit(solution)/shard_map/htd,hde->hte/dot_general | solution.py:57
  153.8 0.0 copy-done.2
  153.8 0.3 fusion.10
  154.1 30.7 %all-gather.4.cloned.1.call-done = bf16[1024,1024]{1,0:T(8,128)(2,1)} async-done(((bf16[512,1024]{1,0:T(8,128)(2,1)}), bf16[1024,1024]{1,0:T(8,128)(2,1)}) %all-gather.4.cloned.1.call-update) | async-done | bytes 2097168 | tf_op jit(solution)/shard_map/all_gather | solution.py:90
  184.8 3.8 %fusion.11 = bf16[1,512,1024]{2,1,0:T(8,128)(2,1)} fusion(bf16[512,1024]{0,1:T(8,128)(2,1)S(1)} %bitcast.64, bf16[1024,1024]{1,0:T(8,128)(2,1)} %all-gather.4.cloned.1.call-done), kind=kOutput, calls=%fused_computation.23 | convolution fusion | flops 1074266112 | bytes 4194304 | tf_op jit(solution)/shard_map/dot_general | solution.py:89
  (3 shorter events, 0.1 us)
Async XLA Ops:
  6.5 11.5 %copy-start = (bf16[1,512,1024]{2,1,0:T(8,128)(2,1)S(1)}, bf16[1,512,1024]{2,1,0:T(8,128)(2,1)}, u32[]{:S(2)}) copy-start(bf16[1,512,1024]{2,1,0:T(8,128)(2,1)} %param.8) | copy-start | bytes 3145732
  6.5 145.1 %all-gather.6.cloned.1.call-start = ((), (), s32[]{:S(2)}) async-start(), calls=%async_computation.1 | async-start | bytes 4456448 | tf_op jit(solution)/shard_map/all_gather | solution.py:27
  15.1 71.4 %collective-permute-start = (bf16[3,1024,512]{1,2,0:T(8,128)(2,1)}, bf16[3,1024,512]{1,2,0:T(8,128)(2,1)}, u32[]{:S(2)}, u32[]{:S(2)}) collective-permute-start(bf16[3,1024,512]{1,2,0:T(8,128)(2,1)} %pad_maximum_fusion), channel_id=1, source_target_pairs={{0,16},{16,0},{1,17},{17,1},{2,18},{18,2},{3,19},{19,3},{4,20},{20... | collective-permute-start | bytes 9437192 | tf_op jit(solution)/shard_map/ppermute | solution.py:15
  97.3 1.1 copy-start.1
  99.6 85.2 %all-gather.4.cloned.1.call-start = ((), (), s32[]{:S(2)}) async-start(), calls=%async_computation | async-start | bytes 3145728 | tf_op jit(solution)/shard_map/all_gather | solution.py:90
  151.7 2.1 %copy-start.2 = (f32[1024]{0:T(1024)S(1)}, f32[1024]{0:T(1024)}, u32[]{:S(2)}) copy-start(f32[1024]{0:T(1024)} %param.13) | copy-start | bytes 12292
Sparse Core Ops, SparseCore 0:
  99.7 51.8 all-gather.5
  153.1 31.6 all-gather.3
